TPU v7x, 32 devices: a whole 2x2x4 slice. The times are simulated.
32 devices in a mesh: space: 4 (over y, x), mode: 8 (over z, core).
Axes of the slice: x: 2, y: 2, z: 4, core: 2. Of those that a mesh axis runs over, the one named last changes fastest.
Arguments:
- source_field: float32 [8, 4, 128, 2048], P('space', None, None, 'mode'), may hold values from -6 to 6
- mean_operator: float32 [8, 4, 128, 896], P('space'), may hold values from -0.109375 to 0.109375
- field_operators: float32 [4, 8, 4, 128, 896], P(None, 'space'), may hold values from -0.078125 to 0.078125
- adjacency: int32 [8, 4, 4], P('space'), may hold values from 0 to 3
- mode_masks: int32 [4], replicated, may hold values from 256 to 1024, as said below
Outputs:
- solution_field: float32 [8, 4, 128, 2048], P('space', None, None, 'mode')
- residual: float32 [8, 4, 128, 2048], P('space', None, None, 'mode')
Inputs may be any that keep to these rules, and one draw needn't show every extreme that they name: `mode_masks`: each value is 256 times a power of two, at most 1024, and every such value belongs to at least one field.
All inputs are finite; a program needn't handle non-finite values.
Results may differ from a plain program's by a relative error of at most 0.0001.
Values sent between devices are 32-bit elements; how exact they have to be, the bound alone decides.
A program may use at most 128 MiB of HBM per device.

v0:
```python
import jax
import jax.numpy as jnp
from jax import lax
from jax.sharding import PartitionSpec as P

DEGREE = 4


coupling_coef = 0.5773502691896258
theta_value = 1.0
delta_value = 0.7


def padded_2(cells, sides, width):
    for axis, dim in sides:
        count = lax.axis_size(axis)
        ends = count - 1
        head = lax.slice_in_dim(cells, 0, width, axis=dim)
        tail = lax.slice_in_dim(cells, cells.shape[dim] - width, cells.shape[dim], axis=dim)
        cells = jnp.concatenate(
            [
                lax.ppermute(tail, axis, [(i, (i + 1) % count) for i in range(ends)]),
                cells,
                lax.ppermute(head, axis, [((i + 1) % count, i) for i in range(ends)]),
            ],
            axis=dim,
        )
    return cells


def swapped(value, axis, distance):
    mask = 2**distance
    pairs = [(source, source ^ mask) for source in range(lax.axis_size(axis))]
    return lax.ppermute(value, axis, pairs)


def gather_columns(padded, adjacency):
    centre = padded[1:-1]
    lower_layer = padded[:-2]
    upper_layer = padded[2:]
    in_layer = jax.vmap(lambda slab_layer, neighbours: slab_layer[neighbours])(centre, adjacency)
    stacked = jnp.concatenate(
        [centre[:, :, None], lower_layer[:, :, None], upper_layer[:, :, None], in_layer], axis=2
    )
    shape_now = centre.shape
    return stacked.reshape(shape_now[0], shape_now[1], 7 * shape_now[2], shape_now[3])


def block_product(operator, columns):
    return jnp.einsum(
        "lfij,lfjm->lfim",
        operator,
        columns,
        precision=lax.Precision.HIGHEST,
        preferred_element_type=jnp.float32,
    )


def per_device(source_field, mean_operator, field_operators, adjacency, mode_masks):
    modes_dev = source_field.shape[3]
    bit_total = lax.axis_size("mode").bit_length() - 1
    selectors = [
        jnp.where(mode_masks == modes_dev * (1 << bit_number), coupling_coef, 0.0).astype(
            jnp.float32
        )
        for bit_number in range(bit_total)
    ]

    def operate_on(field):
        padded = padded_2(field, (("space", 0),), 1)
        columns = gather_columns(padded, adjacency)
        result = field + block_product(mean_operator, columns)
        field_terms = jnp.einsum(
            "jlfik,lfkm->jlfim",
            field_operators,
            columns,
            precision=lax.Precision.HIGHEST,
            preferred_element_type=jnp.float32,
        )
        bit_terms = [
            jnp.einsum("j,jlfim->lfim", selector, field_terms, precision=lax.Precision.HIGHEST)
            for selector in selectors
        ]
        for bit_number in range(bit_total):
            result = result + swapped(bit_terms[bit_number], "mode", bit_number)
        return result

    sigma_value = theta_value / delta_value
    solution_field = jnp.zeros_like(source_field)
    residual = source_field
    direction = source_field / theta_value
    ratio_now = jnp.asarray(1.0 / sigma_value, dtype=jnp.float32)

    def iterate_once(count, carry):
        solution_field, residual, direction, ratio_now = carry
        solution_field = solution_field + direction
        residual = residual - operate_on(direction)
        ratio_new = 1.0 / (2.0 * sigma_value - ratio_now)
        direction = ratio_new * ratio_now * direction + 2.0 * ratio_new / delta_value * residual
        return (solution_field, residual, direction, ratio_new)

    solution_field, residual, direction, ratio_now = lax.fori_loop(
        0, DEGREE, iterate_once, (solution_field, residual, direction, ratio_now)
    )
    return (solution_field, residual)


def solution(mesh):
    in_specs = (
        P("space", None, None, "mode"),
        P("space", None, None, None),
        P(None, "space", None, None, None),
        P("space", None, None),
        P(),
    )
    out_specs = (P("space", None, None, "mode"), P("space", None, None, "mode"))
    return jax.shard_map(
        per_device, mesh=mesh, in_specs=in_specs, out_specs=out_specs, check_vma=False
    )
```

profile of v0, /device:TPU:29, one launch (start us, length us, event | category | flops | bytes accessed | tf_op | source)
XLA Modules:
  0.0 522.7 jit_solution(12654605079831415112)
XLA Ops:
  0.6 0.7 compare_select_fusion.1
  1.3 1.5 copy.24
  2.9 12.0 %copy.26 = f32[4,2,4,128,896]{4,3,0,2,1:T(8,128)} copy(f32[4,2,4,128,896]{4,3,2,1,0:T(8,128)} %param.9) | data formatting | bytes 29360128
  14.9 503.9 %while.19 = (s32[]{:T(128)}, f32[2,4,128,256]{2,3,1,0:T(8,128)}, f32[2,4,128,256]{2,3,1,0:T(8,128)S(1)}, f32[2,4,128,256]{2,3,1,0:T(8,128)S(1)}, f32[]{:T(128)},...) while((s32[]{:T(128)}, f32[2,4,128,256]{2,3,1,0:T(8,128)}, ...), condition=%wide.region_1.2_spmd.clone, body=%wide.region_0.1_spmd.clone.sunk | while | flops 14107017216 | bytes 139986224 | solution.py:102
  15.3 1.1 fusion.31
  16.4 3.1 collective-permute-start
  19.5 3.1 collective-permute-start.1
  22.7 2.9 gather_fusion
  25.5 5.7 %copy.50 = f32[32,128,256]{2,1,0:T(8,128)} copy(f32[32,128,256]{1,2,0:T(8,128)} %gather_fusion) | data formatting | bytes 8388608 | tf_op jit(solution)/shard_map/while/body/eval_jaxpr/vmap()/gather | solution.py:41
  31.2 1.1 collective-permute-done
  32.3 9.3 %collective-permute-done.1 = f32[1,4,128,256]{3,2,1,0:T(8,128)} collective-permute-done((f32[1,4,128,256]{3,2,1,0:T(8,128)}, f32[1,4,128,256]{3,2,1,0:T(8,128)}, u32[]{:S(2)}, u32[]{:S(2)}) %collective-permute-start.1) | collective-permute-done | bytes 524320 | tf_op jit(solution)/shard_map/while/body/eval_jaxpr/ppermute | solution.py:24
  41.6 1.4 fusion.32
  43.0 2.6 pad_maximum_fusion.4
  45.6 32.1 %fusion.33 = (f32[2,4,128,256]{2,3,1,0:T(8,128)}, f32[2,4,128,256]{2,3,1,0:T(8,128)}, f32[2,4,128,256]{2,3,1,0:T(8,128)}) fusion(f32[4]{0:T(128)S(1)} %get-tuple-element.364, f32[4]{0:T(128)S(1)} %get-tuple-element.365, f32[4]{0:T(128)S(1)} %get-tuple-element.366, f32[2,4,896,256,1]{3,2,4,1,0:T(8,128)S(1)} %bitcast.63, ...), kind=kOutput, calls=%fused_computation.5.clone.1 | convolution fusion | flops 11279794176 | bytes 25165872 | tf_op jit(solution)/shard_map/while/body/eval_jaxpr/jlfik,lfkm->jlfim/dot_general | solution.py:73
  77.9 2.1 collective-permute-start.4
  80.0 46.3 %collective-permute-done.2 = f32[2,4,128,256]{2,3,1,0:T(8,128)} collective-permute-done((f32[2,4,128,256]{2,3,1,0:T(8,128)}, f32[2,4,128,256]{2,3,1,0:T(8,128)}, u32[]{:S(2)}, u32[]{:S(2)}) %collective-permute-start.2) | collective-permute-done | bytes 1048608 | tf_op jit(solution)/shard_map/while/body/eval_jaxpr/ppermute | solution.py:34
  126.3 15.8 %multiply_add_fusion.2 = (f32[2,4,128,256]{2,3,1,0:T(8,128)S(1)}, f32[2,4,128,256]{2,3,1,0:T(8,128)S(1)}, f32[2,4,128,256]{2,3,1,0:T(8,128)S(1)}) fusion(f32[2,4,128,256]{2,3,1,0:T(8,128)S(1)} %get-tuple-element.344, f32[]{:T(128)S(6)} %div.16, f32[]{:T(128)S(6)} %mul.49, f32[2,4,128,256]{2,3,1,0:T(8,128)S(1)} %copy-done.1, pred[]{:T(512)S(6)} %compare.3, ...), kind=kOutput, calls=%fused_computation.19.clone.1 | convolution fusion | flops 2821193728 | bytes 20447240 | tf_op jit(solution)/shard_map/while/body/eval_jaxpr/lfij,lfjm->lfim/dot_general | solution.py:50
  142.1 1.0 copy-done.2
  143.4 1.1 fusion.31
  144.5 1.9 collective-permute-start
  146.4 5.0 collective-permute-start.1
  151.5 2.9 gather_fusion
  154.4 5.7 %copy.50 = f32[32,128,256]{2,1,0:T(8,128)} copy(f32[32,128,256]{1,2,0:T(8,128)} %gather_fusion) | data formatting | bytes 8388608 | tf_op jit(solution)/shard_map/while/body/eval_jaxpr/vmap()/gather | solution.py:41
  160.1 1.6 collective-permute-done
  161.6 7.4 %collective-permute-done.1 = f32[1,4,128,256]{3,2,1,0:T(8,128)} collective-permute-done((f32[1,4,128,256]{3,2,1,0:T(8,128)}, f32[1,4,128,256]{3,2,1,0:T(8,128)}, u32[]{:S(2)}, u32[]{:S(2)}) %collective-permute-start.1) | collective-permute-done | bytes 524320 | tf_op jit(solution)/shard_map/while/body/eval_jaxpr/ppermute | solution.py:24
  169.0 1.4 fusion.32
  170.4 2.6 pad_maximum_fusion.4
  173.0 32.1 %fusion.33 = (f32[2,4,128,256]{2,3,1,0:T(8,128)}, f32[2,4,128,256]{2,3,1,0:T(8,128)}, f32[2,4,128,256]{2,3,1,0:T(8,128)}) fusion(f32[4]{0:T(128)S(1)} %get-tuple-element.364, f32[4]{0:T(128)S(1)} %get-tuple-element.365, f32[4]{0:T(128)S(1)} %get-tuple-element.366, f32[2,4,896,256,1]{3,2,4,1,0:T(8,128)S(1)} %bitcast.63, ...), kind=kOutput, calls=%fused_computation.5.clone.1 | convolution fusion | flops 11279794176 | bytes 25165872 | tf_op jit(solution)/shard_map/while/body/eval_jaxpr/jlfik,lfkm->jlfim/dot_general | solution.py:73
  205.1 1.1 collective-permute-start.4
  206.2 43.1 %collective-permute-done.2 = f32[2,4,128,256]{2,3,1,0:T(8,128)} collective-permute-done((f32[2,4,128,256]{2,3,1,0:T(8,128)}, f32[2,4,128,256]{2,3,1,0:T(8,128)}, u32[]{:S(2)}, u32[]{:S(2)}) %collective-permute-start.2) | collective-permute-done | bytes 1048608 | tf_op jit(solution)/shard_map/while/body/eval_jaxpr/ppermute | solution.py:34
  249.3 2.2 collective-permute-done.3
  251.6 15.8 %multiply_add_fusion.2 = (f32[2,4,128,256]{2,3,1,0:T(8,128)S(1)}, f32[2,4,128,256]{2,3,1,0:T(8,128)S(1)}, f32[2,4,128,256]{2,3,1,0:T(8,128)S(1)}) fusion(f32[2,4,128,256]{2,3,1,0:T(8,128)S(1)} %get-tuple-element.344, f32[]{:T(128)S(6)} %div.16, f32[]{:T(128)S(6)} %mul.49, f32[2,4,128,256]{2,3,1,0:T(8,128)S(1)} %copy-done.1, pred[]{:T(512)S(6)} %compare.3, ...), kind=kOutput, calls=%fused_computation.19.clone.1 | convolution fusion | flops 2821193728 | bytes 20447240 | tf_op jit(solution)/shard_map/while/body/eval_jaxpr/lfij,lfjm->lfim/dot_general | solution.py:50
  267.3 1.0 copy-done.2
  268.6 1.1 fusion.31
  269.7 1.9 collective-permute-start
  271.7 5.0 collective-permute-start.1
  276.8 2.9 gather_fusion
  279.6 5.7 %copy.50 = f32[32,128,256]{2,1,0:T(8,128)} copy(f32[32,128,256]{1,2,0:T(8,128)} %gather_fusion) | data formatting | bytes 8388608 | tf_op jit(solution)/shard_map/while/body/eval_jaxpr/vmap()/gather | solution.py:41
  285.5 7.4 %collective-permute-done.1 = f32[1,4,128,256]{3,2,1,0:T(8,128)} collective-permute-done((f32[1,4,128,256]{3,2,1,0:T(8,128)}, f32[1,4,128,256]{3,2,1,0:T(8,128)}, u32[]{:S(2)}, u32[]{:S(2)}) %collective-permute-start.1) | collective-permute-done | bytes 524320 | tf_op jit(solution)/shard_map/while/body/eval_jaxpr/ppermute | solution.py:24
  292.9 1.4 fusion.32
  294.3 2.6 pad_maximum_fusion.4
  296.9 32.0 %fusion.33 = (f32[2,4,128,256]{2,3,1,0:T(8,128)}, f32[2,4,128,256]{2,3,1,0:T(8,128)}, f32[2,4,128,256]{2,3,1,0:T(8,128)}) fusion(f32[4]{0:T(128)S(1)} %get-tuple-element.364, f32[4]{0:T(128)S(1)} %get-tuple-element.365, f32[4]{0:T(128)S(1)} %get-tuple-element.366, f32[2,4,896,256,1]{3,2,4,1,0:T(8,128)S(1)} %bitcast.63, ...), kind=kOutput, calls=%fused_computation.5.clone.1 | convolution fusion | flops 11279794176 | bytes 25165872 | tf_op jit(solution)/shard_map/while/body/eval_jaxpr/jlfik,lfkm->jlfim/dot_general | solution.py:73
  328.9 0.6 collective-permute-start.3
  329.5 2.5 collective-permute-start.4
  332.0 45.4 %collective-permute-done.2 = f32[2,4,128,256]{2,3,1,0:T(8,128)} collective-permute-done((f32[2,4,128,256]{2,3,1,0:T(8,128)}, f32[2,4,128,256]{2,3,1,0:T(8,128)}, u32[]{:S(2)}, u32[]{:S(2)}) %collective-permute-start.2) | collective-permute-done | bytes 1048608 | tf_op jit(solution)/shard_map/while/body/eval_jaxpr/ppermute | solution.py:34
  377.4 15.8 %multiply_add_fusion.2 = (f32[2,4,128,256]{2,3,1,0:T(8,128)S(1)}, f32[2,4,128,256]{2,3,1,0:T(8,128)S(1)}, f32[2,4,128,256]{2,3,1,0:T(8,128)S(1)}) fusion(f32[2,4,128,256]{2,3,1,0:T(8,128)S(1)} %get-tuple-element.344, f32[]{:T(128)S(6)} %div.16, f32[]{:T(128)S(6)} %mul.49, f32[2,4,128,256]{2,3,1,0:T(8,128)S(1)} %copy-done.1, pred[]{:T(512)S(6)} %compare.3, ...), kind=kOutput, calls=%fused_computation.19.clone.1 | convolution fusion | flops 2821193728 | bytes 20447240 | tf_op jit(solution)/shard_map/while/body/eval_jaxpr/lfij,lfjm->lfim/dot_general | solution.py:50
  393.2 1.0 copy-done.2
  394.5 1.1 fusion.31
  395.6 1.9 collective-permute-start
  397.5 5.0 collective-permute-start.1
  402.6 2.9 gather_fusion
  405.5 5.7 %copy.50 = f32[32,128,256]{2,1,0:T(8,128)} copy(f32[32,128,256]{1,2,0:T(8,128)} %gather_fusion) | data formatting | bytes 8388608 | tf_op jit(solution)/shard_map/while/body/eval_jaxpr/vmap()/gather | solution.py:41
  411.1 1.3 collective-permute-done
  412.4 7.4 %collective-permute-done.1 = f32[1,4,128,256]{3,2,1,0:T(8,128)} collective-permute-done((f32[1,4,128,256]{3,2,1,0:T(8,128)}, f32[1,4,128,256]{3,2,1,0:T(8,128)}, u32[]{:S(2)}, u32[]{:S(2)}) %collective-permute-start.1) | collective-permute-done | bytes 524320 | tf_op jit(solution)/shard_map/while/body/eval_jaxpr/ppermute | solution.py:24
  419.8 1.4 fusion.32
  421.2 2.6 pad_maximum_fusion.4
  423.8 32.1 %fusion.33 = (f32[2,4,128,256]{2,3,1,0:T(8,128)}, f32[2,4,128,256]{2,3,1,0:T(8,128)}, f32[2,4,128,256]{2,3,1,0:T(8,128)}) fusion(f32[4]{0:T(128)S(1)} %get-tuple-element.364, f32[4]{0:T(128)S(1)} %get-tuple-element.365, f32[4]{0:T(128)S(1)} %get-tuple-element.366, f32[2,4,896,256,1]{3,2,4,1,0:T(8,128)S(1)} %bitcast.63, ...), kind=kOutput, calls=%fused_computation.5.clone.1 | convolution fusion | flops 11279794176 | bytes 25165872 | tf_op jit(solution)/shard_map/while/body/eval_jaxpr/jlfik,lfkm->jlfim/dot_general | solution.py:73
  455.9 2.2 collective-permute-start.4
  458.1 43.2 %collective-permute-done.2 = f32[2,4,128,256]{2,3,1,0:T(8,128)} collective-permute-done((f32[2,4,128,256]{2,3,1,0:T(8,128)}, f32[2,4,128,256]{2,3,1,0:T(8,128)}, u32[]{:S(2)}, u32[]{:S(2)}) %collective-permute-start.2) | collective-permute-done | bytes 1048608 | tf_op jit(solution)/shard_map/while/body/eval_jaxpr/ppermute | solution.py:34
  501.3 0.8 collective-permute-done.3
  502.1 15.8 %multiply_add_fusion.2 = (f32[2,4,128,256]{2,3,1,0:T(8,128)S(1)}, f32[2,4,128,256]{2,3,1,0:T(8,128)S(1)}, f32[2,4,128,256]{2,3,1,0:T(8,128)S(1)}) fusion(f32[2,4,128,256]{2,3,1,0:T(8,128)S(1)} %get-tuple-element.344, f32[]{:T(128)S(6)} %div.16, f32[]{:T(128)S(6)} %mul.49, f32[2,4,128,256]{2,3,1,0:T(8,128)S(1)} %copy-done.1, pred[]{:T(512)S(6)} %compare.3, ...), kind=kOutput, calls=%fused_computation.19.clone.1 | convolution fusion | flops 2821193728 | bytes 20447240 | tf_op jit(solution)/shard_map/while/body/eval_jaxpr/lfij,lfjm->lfim/dot_general | solution.py:50
  517.9 1.0 copy-done.2
  518.8 2.5 copy.27
  521.4 1.3 copy.28
  (50 shorter events, 2.3 us)
Async XLA Ops:
  2.9 12.0 %copy-start.3 = (s32[2,4,4]{2,1,0:T(4,128)S(1)}, s32[2,4,4]{2,1,0:T(4,128)}, u32[]{:S(2)}) copy-start(s32[2,4,4]{2,1,0:T(4,128)} %param.10) | copy-start | bytes 388
  16.4 15.9 %collective-permute-start = (f32[1,4,128,256]{3,2,1,0:T(8,128)}, f32[1,4,128,256]{3,2,1,0:T(8,128)}, u32[]{:S(2)}, u32[]{:S(2)}) collective-permute-start(f32[1,4,128,256]{3,2,1,0:T(8,128)} %get-tuple-element.316), channel_id=1, source_target_pairs={{0,8},{8,16},{16,24},{1,9},{9,17},{17,25},{2,10},{10,18},{18,26},{... | collective-permute-start | bytes 1572872 | tf_op jit(solution)/shard_map/while/body/eval_jaxpr/ppermute | solution.py:22
  19.5 22.1 %collective-permute-start.1 = (f32[1,4,128,256]{3,2,1,0:T(8,128)}, f32[1,4,128,256]{3,2,1,0:T(8,128)}, u32[]{:S(2)}, u32[]{:S(2)}) collective-permute-start(f32[1,4,128,256]{3,2,1,0:T(8,128)} %get-tuple-element.317), channel_id=1, source_target_pairs={{8,0},{16,8},{24,16},{9,1},{17,9},{25,17},{10,2},{18,10},{26,18},{... | collective-permute-start | bytes 1572872 | tf_op jit(solution)/shard_map/while/body/eval_jaxpr/ppermute | solution.py:24
  45.6 32.1 %copy-start = (f32[2,4,7,128,256]{4,3,2,1,0:T(8,128)}, f32[2,4,7,128,256]{4,3,2,1,0:T(8,128)S(1)}, u32[]{:S(2)}) copy-start(f32[2,4,7,128,256]{4,3,2,1,0:T(8,128)S(1)} %pad_maximum_fusion.4) | copy-start | bytes 22020100 | tf_op jit(solution)/shard_map/while
  45.6 80.7 %copy-start.1 = (f32[2,4,128,256]{2,3,1,0:T(8,128)S(1)}, f32[2,4,128,256]{2,3,1,0:T(8,128)}, u32[]{:S(2)}) copy-start(f32[2,4,128,256]{2,3,1,0:T(8,128)} %get-tuple-element.342) | copy-start | bytes 3145732 | tf_op jit(solution)/shard_map/while
  77.7 48.7 %collective-permute-start.2 = (f32[2,4,128,256]{2,3,1,0:T(8,128)}, f32[2,4,128,256]{2,3,1,0:T(8,128)}, u32[]{:S(2)}, u32[]{:S(2)}) collective-permute-start(f32[2,4,128,256]{2,3,1,0:T(8,128)} %get-tuple-element.320), channel_id=1, source_target_pairs={{0,4},{1,5},{2,6},{3,7},{4,0},{5,1},{6,2},{7,3},{8,12},{9,13},{10,... | collective-permute-start | bytes 3145736 | tf_op jit(solution)/shard_map/while/body/eval_jaxpr/ppermute | solution.py:34
  77.7 48.6 %collective-permute-start.3 = (f32[2,4,128,256]{2,3,1,0:T(8,128)}, f32[2,4,128,256]{2,3,1,0:T(8,128)}, u32[]{:S(2)}, u32[]{:S(2)}) collective-permute-start(f32[2,4,128,256]{2,3,1,0:T(8,128)} %get-tuple-element.321), channel_id=1, source_target_pairs={{0,2},{1,3},{2,0},{3,1},{4,6},{5,7},{6,4},{7,5},{8,10},{9,11},{10,... | collective-permute-start | bytes 3145736 | tf_op jit(solution)/shard_map/while/body/eval_jaxpr/ppermute | solution.py:34
  77.9 48.4 %collective-permute-start.4 = (f32[2,4,128,256]{2,3,1,0:T(8,128)}, f32[2,4,128,256]{2,3,1,0:T(8,128)}, u32[]{:S(2)}, u32[]{:S(2)}) collective-permute-start(f32[2,4,128,256]{2,3,1,0:T(8,128)} %get-tuple-element.322), channel_id=1, source_target_pairs={{0,1},{1,0},{2,3},{3,2},{4,5},{5,4},{6,7},{7,6},{8,9},{9,8},{10,11... | collective-permute-start | bytes 3145736 | tf_op jit(solution)/shard_map/while/body/eval_jaxpr/ppermute | solution.py:34
  142.1 1.0 copy-start.2
  144.5 17.1 %collective-permute-start = (f32[1,4,128,256]{3,2,1,0:T(8,128)}, f32[1,4,128,256]{3,2,1,0:T(8,128)}, u32[]{:S(2)}, u32[]{:S(2)}) collective-permute-start(f32[1,4,128,256]{3,2,1,0:T(8,128)} %get-tuple-element.316), channel_id=1, source_target_pairs={{0,8},{8,16},{16,24},{1,9},{9,17},{17,25},{2,10},{10,18},{18,26},{... | collective-permute-start | bytes 1572872 | tf_op jit(solution)/shard_map/while/body/eval_jaxpr/ppermute | solution.py:22
  146.4 22.6 %collective-permute-start.1 = (f32[1,4,128,256]{3,2,1,0:T(8,128)}, f32[1,4,128,256]{3,2,1,0:T(8,128)}, u32[]{:S(2)}, u32[]{:S(2)}) collective-permute-start(f32[1,4,128,256]{3,2,1,0:T(8,128)} %get-tuple-element.317), channel_id=1, source_target_pairs={{8,0},{16,8},{24,16},{9,1},{17,9},{25,17},{10,2},{18,10},{26,18},{... | collective-permute-start | bytes 1572872 | tf_op jit(solution)/shard_map/while/body/eval_jaxpr/ppermute | solution.py:24
  173.0 32.1 %copy-start = (f32[2,4,7,128,256]{4,3,2,1,0:T(8,128)}, f32[2,4,7,128,256]{4,3,2,1,0:T(8,128)S(1)}, u32[]{:S(2)}) copy-start(f32[2,4,7,128,256]{4,3,2,1,0:T(8,128)S(1)} %pad_maximum_fusion.4) | copy-start | bytes 22020100 | tf_op jit(solution)/shard_map/while
  173.0 78.6 %copy-start.1 = (f32[2,4,128,256]{2,3,1,0:T(8,128)S(1)}, f32[2,4,128,256]{2,3,1,0:T(8,128)}, u32[]{:S(2)}) copy-start(f32[2,4,128,256]{2,3,1,0:T(8,128)} %get-tuple-element.342) | copy-start | bytes 3145732 | tf_op jit(solution)/shard_map/while
  205.1 44.3 %collective-permute-start.2 = (f32[2,4,128,256]{2,3,1,0:T(8,128)}, f32[2,4,128,256]{2,3,1,0:T(8,128)}, u32[]{:S(2)}, u32[]{:S(2)}) collective-permute-start(f32[2,4,128,256]{2,3,1,0:T(8,128)} %get-tuple-element.320), channel_id=1, source_target_pairs={{0,4},{1,5},{2,6},{3,7},{4,0},{5,1},{6,2},{7,3},{8,12},{9,13},{10,... | collective-permute-start | bytes 3145736 | tf_op jit(solution)/shard_map/while/body/eval_jaxpr/ppermute | solution.py:34
  205.1 46.5 %collective-permute-start.3 = (f32[2,4,128,256]{2,3,1,0:T(8,128)}, f32[2,4,128,256]{2,3,1,0:T(8,128)}, u32[]{:S(2)}, u32[]{:S(2)}) collective-permute-start(f32[2,4,128,256]{2,3,1,0:T(8,128)} %get-tuple-element.321), channel_id=1, source_target_pairs={{0,2},{1,3},{2,0},{3,1},{4,6},{5,7},{6,4},{7,5},{8,10},{9,11},{10,... | collective-permute-start | bytes 3145736 | tf_op jit(solution)/shard_map/while/body/eval_jaxpr/ppermute | solution.py:34
  205.1 46.5 %collective-permute-start.4 = (f32[2,4,128,256]{2,3,1,0:T(8,128)}, f32[2,4,128,256]{2,3,1,0:T(8,128)}, u32[]{:S(2)}, u32[]{:S(2)}) collective-permute-start(f32[2,4,128,256]{2,3,1,0:T(8,128)} %get-tuple-element.322), channel_id=1, source_target_pairs={{0,1},{1,0},{2,3},{3,2},{4,5},{5,4},{6,7},{7,6},{8,9},{9,8},{10,11... | collective-permute-start | bytes 3145736 | tf_op jit(solution)/shard_map/while/body/eval_jaxpr/ppermute | solution.py:34
  267.3 1.0 copy-start.2
  269.7 15.7 %collective-permute-start = (f32[1,4,128,256]{3,2,1,0:T(8,128)}, f32[1,4,128,256]{3,2,1,0:T(8,128)}, u32[]{:S(2)}, u32[]{:S(2)}) collective-permute-start(f32[1,4,128,256]{3,2,1,0:T(8,128)} %get-tuple-element.316), channel_id=1, source_target_pairs={{0,8},{8,16},{16,24},{1,9},{9,17},{17,25},{2,10},{10,18},{18,26},{... | collective-permute-start | bytes 1572872 | tf_op jit(solution)/shard_map/while/body/eval_jaxpr/ppermute | solution.py:22
  271.7 21.2 %collective-permute-start.1 = (f32[1,4,128,256]{3,2,1,0:T(8,128)}, f32[1,4,128,256]{3,2,1,0:T(8,128)}, u32[]{:S(2)}, u32[]{:S(2)}) collective-permute-start(f32[1,4,128,256]{3,2,1,0:T(8,128)} %get-tuple-element.317), channel_id=1, source_target_pairs={{8,0},{16,8},{24,16},{9,1},{17,9},{25,17},{10,2},{18,10},{26,18},{... | collective-permute-start | bytes 1572872 | tf_op jit(solution)/shard_map/while/body/eval_jaxpr/ppermute | solution.py:24
  296.8 32.1 %copy-start = (f32[2,4,7,128,256]{4,3,2,1,0:T(8,128)}, f32[2,4,7,128,256]{4,3,2,1,0:T(8,128)S(1)}, u32[]{:S(2)}) copy-start(f32[2,4,7,128,256]{4,3,2,1,0:T(8,128)S(1)} %pad_maximum_fusion.4) | copy-start | bytes 22020100 | tf_op jit(solution)/shard_map/while
  296.8 80.5 %copy-start.1 = (f32[2,4,128,256]{2,3,1,0:T(8,128)S(1)}, f32[2,4,128,256]{2,3,1,0:T(8,128)}, u32[]{:S(2)}) copy-start(f32[2,4,128,256]{2,3,1,0:T(8,128)} %get-tuple-element.342) | copy-start | bytes 3145732 | tf_op jit(solution)/shard_map/while
  328.9 48.5 %collective-permute-start.2 = (f32[2,4,128,256]{2,3,1,0:T(8,128)}, f32[2,4,128,256]{2,3,1,0:T(8,128)}, u32[]{:S(2)}, u32[]{:S(2)}) collective-permute-start(f32[2,4,128,256]{2,3,1,0:T(8,128)} %get-tuple-element.320), channel_id=1, source_target_pairs={{0,4},{1,5},{2,6},{3,7},{4,0},{5,1},{6,2},{7,3},{8,12},{9,13},{10,... | collective-permute-start | bytes 3145736 | tf_op jit(solution)/shard_map/while/body/eval_jaxpr/ppermute | solution.py:34
  328.9 48.5 %collective-permute-start.3 = (f32[2,4,128,256]{2,3,1,0:T(8,128)}, f32[2,4,128,256]{2,3,1,0:T(8,128)}, u32[]{:S(2)}, u32[]{:S(2)}) collective-permute-start(f32[2,4,128,256]{2,3,1,0:T(8,128)} %get-tuple-element.321), channel_id=1, source_target_pairs={{0,2},{1,3},{2,0},{3,1},{4,6},{5,7},{6,4},{7,5},{8,10},{9,11},{10,... | collective-permute-start | bytes 3145736 | tf_op jit(solution)/shard_map/while/body/eval_jaxpr/ppermute | solution.py:34
  329.5 47.9 %collective-permute-start.4 = (f32[2,4,128,256]{2,3,1,0:T(8,128)}, f32[2,4,128,256]{2,3,1,0:T(8,128)}, u32[]{:S(2)}, u32[]{:S(2)}) collective-permute-start(f32[2,4,128,256]{2,3,1,0:T(8,128)} %get-tuple-element.322), channel_id=1, source_target_pairs={{0,1},{1,0},{2,3},{3,2},{4,5},{5,4},{6,7},{7,6},{8,9},{9,8},{10,11... | collective-permute-start | bytes 3145736 | tf_op jit(solution)/shard_map/while/body/eval_jaxpr/ppermute | solution.py:34
  393.2 1.0 copy-start.2
  395.6 16.8 %collective-permute-start = (f32[1,4,128,256]{3,2,1,0:T(8,128)}, f32[1,4,128,256]{3,2,1,0:T(8,128)}, u32[]{:S(2)}, u32[]{:S(2)}) collective-permute-start(f32[1,4,128,256]{3,2,1,0:T(8,128)} %get-tuple-element.316), channel_id=1, source_target_pairs={{0,8},{8,16},{16,24},{1,9},{9,17},{17,25},{2,10},{10,18},{18,26},{... | collective-permute-start | bytes 1572872 | tf_op jit(solution)/shard_map/while/body/eval_jaxpr/ppermute | solution.py:22
  397.5 22.3 %collective-permute-start.1 = (f32[1,4,128,256]{3,2,1,0:T(8,128)}, f32[1,4,128,256]{3,2,1,0:T(8,128)}, u32[]{:S(2)}, u32[]{:S(2)}) collective-permute-start(f32[1,4,128,256]{3,2,1,0:T(8,128)} %get-tuple-element.317), channel_id=1, source_target_pairs={{8,0},{16,8},{24,16},{9,1},{17,9},{25,17},{10,2},{18,10},{26,18},{... | collective-permute-start | bytes 1572872 | tf_op jit(solution)/shard_map/while/body/eval_jaxpr/ppermute | solution.py:24
  423.8 32.1 %copy-start = (f32[2,4,7,128,256]{4,3,2,1,0:T(8,128)}, f32[2,4,7,128,256]{4,3,2,1,0:T(8,128)S(1)}, u32[]{:S(2)}) copy-start(f32[2,4,7,128,256]{4,3,2,1,0:T(8,128)S(1)} %pad_maximum_fusion.4) | copy-start | bytes 22020100 | tf_op jit(solution)/shard_map/while
  423.8 78.3 %copy-start.1 = (f32[2,4,128,256]{2,3,1,0:T(8,128)S(1)}, f32[2,4,128,256]{2,3,1,0:T(8,128)}, u32[]{:S(2)}) copy-start(f32[2,4,128,256]{2,3,1,0:T(8,128)} %get-tuple-element.342) | copy-start | bytes 3145732 | tf_op jit(solution)/shard_map/while
  455.8 45.5 %collective-permute-start.2 = (f32[2,4,128,256]{2,3,1,0:T(8,128)}, f32[2,4,128,256]{2,3,1,0:T(8,128)}, u32[]{:S(2)}, u32[]{:S(2)}) collective-permute-start(f32[2,4,128,256]{2,3,1,0:T(8,128)} %get-tuple-element.320), channel_id=1, source_target_pairs={{0,4},{1,5},{2,6},{3,7},{4,0},{5,1},{6,2},{7,3},{8,12},{9,13},{10,... | collective-permute-start | bytes 3145736 | tf_op jit(solution)/shard_map/while/body/eval_jaxpr/ppermute | solution.py:34
  455.8 46.2 %collective-permute-start.3 = (f32[2,4,128,256]{2,3,1,0:T(8,128)}, f32[2,4,128,256]{2,3,1,0:T(8,128)}, u32[]{:S(2)}, u32[]{:S(2)}) collective-permute-start(f32[2,4,128,256]{2,3,1,0:T(8,128)} %get-tuple-element.321), channel_id=1, source_target_pairs={{0,2},{1,3},{2,0},{3,1},{4,6},{5,7},{6,4},{7,5},{8,10},{9,11},{10,... | collective-permute-start | bytes 3145736 | tf_op jit(solution)/shard_map/while/body/eval_jaxpr/ppermute | solution.py:34
  455.9 46.2 %collective-permute-start.4 = (f32[2,4,128,256]{2,3,1,0:T(8,128)}, f32[2,4,128,256]{2,3,1,0:T(8,128)}, u32[]{:S(2)}, u32[]{:S(2)}) collective-permute-start(f32[2,4,128,256]{2,3,1,0:T(8,128)} %get-tuple-element.322), channel_id=1, source_target_pairs={{0,1},{1,0},{2,3},{3,2},{4,5},{5,4},{6,7},{7,6},{8,9},{9,8},{10,11... | collective-permute-start | bytes 3145736 | tf_op jit(solution)/shard_map/while/body/eval_jaxpr/ppermute | solution.py:34
  517.9 1.0 copy-start.2
where the time goes:
time: 530 us; the launch traced here: 523 us
  waiting for transfers between devices  217 us (41%)
  matrix products  191 us (36%)
  local copies, waits for them, and re-layouts  61.4 us (12%)
  starting transfers between devices  35.6 us (7%)
  other arithmetic  16.4 us (3%)
    ppermute x12, waiting for transfers between devices, swapped(): return lax.ppermute(value, axis, pairs)  181 us
    dot_general x4, matrix products, operate_on(): jnp.einsum('jlfik,lfkm->jlfim', field_operators, columns, precision=lax.P...  128 us
    dot_general x4, matrix products, block_product(): jnp.einsum('lfij,lfjm->lfim', operator, columns, precision=lax.Precision....  63.1 us
    gather x12, local copies, waits for them, and re-layouts, gather_columns(): slab_layer[neighbours]  34.4 us
    ppermute x4, waiting for transfers between devices, padded_2(): lax.ppermute(head, axis, [((i + 1) % count, i) for i in range(ends)])  31.5 us
    ppermute x4, starting transfers between devices, padded_2(): lax.ppermute(head, axis, [((i + 1) % count, i) for i in range(ends)])  18.1 us
    unnamed x7, local copies, waits for them, and re-layouts  17.5 us
  transfers between devices with their start and end apart: 20, of which 14 were waited for; matrix products, arithmetic and copies ran while one was open for 7% of the time, Pallas kernels for 0%

commit v1 on v0

v1 whole, which is shorter than its diff:
```python
import functools

import jax
import jax.numpy as jnp
from jax import lax
from jax.experimental import pallas as pl
from jax.experimental.pallas import tpu as pltpu
from jax.sharding import PartitionSpec as P

DEGREE = 4
COUPLING = 0.5773502691896258
THETA = 1.0
DELTA = 0.7
CHUNKS = 2
VMEM_LIMIT = 66_000_000
MESH = pl.DeviceIdType.MESH


def prep_kernel(face, bits, modes_dev, mean_ref, field_ref, adj_ref, mask_ref, hi_ref, lo_ref):
    layer, f = pl.program_id(0), pl.program_id(1)
    blk = mean_ref.shape[2]
    fields = field_ref.shape[0]
    for op in range(bits + 1):
        if op == 0:
            whole = mean_ref[0, 0]
        else:
            whole = jnp.zeros(mean_ref.shape[2:], jnp.float32)
            for j in range(fields):
                weight = jnp.where(mask_ref[j] == modes_dev * (1 << (op - 1)), COUPLING, 0.0).astype(jnp.float32)
                whole = whole + weight * field_ref[j, 0, 0]
        block = lambda s: whole[:, s * blk : (s + 1) * blk]
        parts = []
        for g in range(face):
            total = jnp.where(f == g, 1.0, 0.0).astype(jnp.float32) * block(0)
            for s in range(adj_ref.shape[2]):
                here = jnp.where(adj_ref[layer, f, s] == g, 1.0, 0.0).astype(jnp.float32)
                total = total + here * block(3 + s)
            parts.append(total)
        parts += [block(1), block(2)]
        for at, part in enumerate(parts):
            high = part.astype(jnp.bfloat16)
            low = (part - high.astype(jnp.float32)).astype(jnp.bfloat16)
            hi_ref[0, 0, op * blk : (op + 1) * blk, at * blk : (at + 1) * blk] = high
            lo_ref[0, 0, op * blk : (op + 1) * blk, at * blk : (at + 1) * blk] = low


def prepared(mean_operator, field_operators, adjacency, mode_masks, bits, modes_dev):
    layers, face, blk, wide = mean_operator.shape
    fields = field_operators.shape[0]
    shape = (layers, face, (bits + 1) * blk, (face + 2) * blk)
    out = jax.ShapeDtypeStruct(shape, jnp.bfloat16)
    spec = pl.BlockSpec((1, 1) + shape[2:], lambda l, f: (l, f, 0, 0))
    return pl.pallas_call(
        functools.partial(prep_kernel, face, bits, modes_dev),
        grid=(layers, face),
        in_specs=[
            pl.BlockSpec((1, 1, blk, wide), lambda l, f: (l, f, 0, 0)),
            pl.BlockSpec((fields, 1, 1, blk, wide), lambda l, f: (0, l, f, 0, 0)),
            pl.BlockSpec(memory_space=pltpu.SMEM),
            pl.BlockSpec(memory_space=pltpu.SMEM),
        ],
        out_specs=(spec, spec),
        out_shape=(out, out),
        compiler_params=pltpu.CompilerParams(vmem_limit_bytes=VMEM_LIMIT),
    )(mean_operator, field_operators, adjacency, mode_masks)


def solve_kernel(
    peers, spaces, chunks, src, hi_hbm, lo_hbm, x_out, r_out,
    w_hi, w_lo, direction, res, x, split, halo_low, halo_up,
    w_sem, own_sem, in_send, in_recv, low_send, low_recv, up_send, up_recv, out_send, out_recv, own_out,
):
    layers, face = w_hi.shape[:2]
    blk = w_hi.shape[2] // (peers.bit_length())
    bits = peers.bit_length() - 1
    lc = src.shape[3]
    rows = peers * lc
    me = lax.axis_index("mode")
    s = lax.axis_index("space")
    has_low = s > 0
    has_up = s < spaces - 1

    load_hi = pltpu.make_async_copy(hi_hbm, w_hi, w_sem.at[0])
    load_lo = pltpu.make_async_copy(lo_hbm, w_lo, w_sem.at[1])
    load_hi.start()
    load_lo.start()

    barrier = pltpu.get_barrier_semaphore()
    for k in range(1, peers):
        pl.semaphore_signal(barrier, inc=1, device_id={"mode": lax.rem(me + k, peers)}, device_id_type=MESH)

    @pl.when(has_low)
    def _():
        pl.semaphore_signal(barrier, inc=1, device_id={"space": s - 1}, device_id_type=MESH)

    @pl.when(has_up)
    def _():
        pl.semaphore_signal(barrier, inc=1, device_id={"space": s + 1}, device_id_type=MESH)

    pl.semaphore_wait(barrier, peers - 1 + has_low.astype(jnp.int32) + has_up.astype(jnp.int32))

    def slab(ref, c, h):
        return ref.at[c, :, pl.ds(pl.multiple_of(h * lc, lc), lc), :]

    def in_copy(c, k):
        to = lax.rem(me + k, peers)
        return pltpu.make_async_remote_copy(
            src_ref=src.at[to, c], dst_ref=slab(direction.at[0], c, me),
            send_sem=in_send.at[c, k], recv_sem=in_recv.at[c, k],
            device_id={"mode": to}, device_id_type=MESH,
        )

    def in_wait(c, k):
        pltpu.make_async_remote_copy(
            src_ref=src.at[0, c], dst_ref=slab(direction.at[0], c, lax.rem(me + peers - k, peers)),
            send_sem=in_send.at[c, k], recv_sem=in_recv.at[c, k],
            device_id={"mode": lax.rem(me + k, peers)}, device_id_type=MESH,
        ).wait_recv()

    def own_copy(c):
        return pltpu.make_async_copy(src.at[me, c], slab(direction.at[0], c, me), own_sem.at[c])

    def to_low(t, c):
        return pltpu.make_async_remote_copy(
            src_ref=direction.at[lax.rem(t, 2), c, 0], dst_ref=halo_up.at[t, c],
            send_sem=low_send.at[t, c], recv_sem=up_recv.at[t, c],
            device_id={"space": s - 1}, device_id_type=MESH,
        )

    def to_up(t, c):
        return pltpu.make_async_remote_copy(
            src_ref=direction.at[lax.rem(t, 2), c, layers - 1], dst_ref=halo_low.at[t, c],
            send_sem=up_send.at[t, c], recv_sem=low_recv.at[t, c],
            device_id={"space": s + 1}, device_id_type=MESH,
        )

    def halo_start(t, c):
        @pl.when(has_low)
        def _():
            to_low(t, c).start()

        @pl.when(has_up)
        def _():
            to_up(t, c).start()

    def halo_sent(t, c):
        @pl.when(has_low)
        def _():
            to_low(t, c).wait_send()

        @pl.when(has_up)
        def _():
            to_up(t, c).wait_send()

    def halo_arrived(t, c):
        @pl.when(has_low)
        def _():
            to_up(t, c).wait_recv()

        @pl.when(has_up)
        def _():
            to_low(t, c).wait_recv()

    def out_copy(which, ref, out, c, k):
        to = lax.rem(me + k, peers)
        return pltpu.make_async_remote_copy(
            src_ref=slab(ref, c, to), dst_ref=out.at[me, c],
            send_sem=out_send.at[which, c, k], recv_sem=out_recv.at[which, c, k],
            device_id={"mode": to}, device_id_type=MESH,
        )

    def out_own(which, ref, out, c):
        return pltpu.make_async_copy(slab(ref, c, me), out.at[me, c], own_out.at[which, c])

    def out_start(which, ref, out, c):
        for k in range(1, peers):
            out_copy(which, ref, out, c, k).start()
        out_own(which, ref, out, c).start()

    def out_finish(which, ref, out, c):
        for k in range(1, peers):
            came = lax.rem(me + peers - k, peers)
            out_copy(which, ref, out, c, k).wait_send()
            pltpu.make_async_remote_copy(
                src_ref=slab(ref, c, me), dst_ref=out.at[came, c],
                send_sem=out_send.at[which, c, k], recv_sem=out_recv.at[which, c, k],
                device_id={"mode": lax.rem(me + k, peers)}, device_id_type=MESH,
            ).wait_recv()
        out_own(which, ref, out, c).wait()

    for c in range(chunks):
        for k in range(1, peers):
            in_copy(c, k).start()
        own_copy(c).start()

    @pl.when(jnp.logical_not(has_low))
    def _():
        halo_low[...] = jnp.zeros_like(halo_low)

    @pl.when(jnp.logical_not(has_up))
    def _():
        halo_up[...] = jnp.zeros_like(halo_up)

    for c in range(chunks):
        own_copy(c).wait()
        for k in range(1, peers):
            in_wait(c, k)
        halo_start(0, c)
        res[c] = direction[0, c]
        x[c] = direction[0, c]
    load_hi.wait()
    load_lo.wait()

    def keep_split(at, value):
        high = value.astype(jnp.bfloat16)
        split[at, :rows, :] = high
        split[at, rows:, :] = (value - high.astype(jnp.float32)).astype(jnp.bfloat16)

    def product(a, b):
        return lax.dot_general(a, b, (((1,), (1,)), ((), ())), preferred_element_type=jnp.float32)

    sigma = THETA / DELTA

    def step(i, ratio):
        t, c = i // chunks, lax.rem(i, chunks)
        now = lax.rem(t, 2)
        ratio_new = 1.0 / (2.0 * sigma - ratio)
        keep, add = ratio_new * ratio, 2.0 * ratio_new / DELTA
        for l in range(layers):
            keep_split(l + 1, direction[now, c, l])
        halo_arrived(t, c)
        keep_split(0, halo_low[t, c])
        keep_split(layers + 1, halo_up[t, c])

        @pl.when(t > 0)
        def _():
            halo_sent(t - 1, c)

        for l in range(layers):
            for f in range(face):
                lanes = slice(f * blk, (f + 1) * blk)
                a = jnp.concatenate([split[l + 1], split[l, :, lanes], split[l + 2, :, lanes]], axis=1)
                y = product(a, w_hi[l, f])
                y = y[:rows] + y[rows:] + product(a[:rows], w_lo[l, f])
                d = direction[now, c, l, :, lanes]
                total = d + y[:, :blk]
                for b in range(bits):
                    term = y[:, (b + 1) * blk : (b + 2) * blk]
                    total = total + jnp.concatenate(
                        [term[(h ^ (1 << b)) * lc : ((h ^ (1 << b)) + 1) * lc] for h in range(peers)], axis=0
                    )
                r = res[c, l, :, lanes] - total
                res[c, l, :, lanes] = r

                @pl.when(t < DEGREE - 1)
                def _():
                    d_new = keep * d + add * r
                    direction[1 - now, c, l, :, lanes] = d_new
                    x[c, l, :, lanes] = x[c, l, :, lanes] + d_new

        @pl.when(t < DEGREE - 1)
        def _():
            halo_start(t + 1, c)

        @pl.when(t == DEGREE - 2)
        def _():
            out_start(0, x, x_out, c)

        @pl.when(t == DEGREE - 1)
        def _():
            out_start(1, res, r_out, c)

        return jnp.where(c == chunks - 1, ratio_new, ratio)

    lax.fori_loop(0, DEGREE * chunks, step, jnp.float32(1.0 / sigma))

    for c in range(chunks):
        halo_sent(DEGREE - 1, c)
        for k in range(1, peers):
            in_copy(c, k).wait_send()
    for c in range(chunks):
        out_finish(0, x, x_out, c)
        out_finish(1, res, r_out, c)


def per_device(peers, spaces, source_field, mean_operator, field_operators, adjacency, mode_masks):
    layers, face, blk, modes_dev = source_field.shape
    bits = peers.bit_length() - 1
    chunks = CHUNKS
    lc = modes_dev // (peers * chunks)
    rows = peers * lc
    wide = face * blk
    w_hi, w_lo = prepared(mean_operator, field_operators, adjacency, mode_masks, bits, modes_dev)
    src = source_field.reshape(layers, face, blk, peers, chunks, lc)
    src = src.transpose(3, 4, 0, 5, 1, 2).reshape(peers, chunks, layers, lc, wide) / THETA
    out = jax.ShapeDtypeStruct(src.shape, jnp.float32)
    field = pltpu.VMEM((chunks, layers, rows, wide), jnp.float32)
    halo = pltpu.VMEM((DEGREE, chunks, rows, wide), jnp.float32)
    dma = pltpu.SemaphoreType.DMA
    x, r = pl.pallas_call(
        functools.partial(solve_kernel, peers, spaces, chunks),
        in_specs=[
            pl.BlockSpec(memory_space=pltpu.VMEM),
            pl.BlockSpec(memory_space=pl.ANY),
            pl.BlockSpec(memory_space=pl.ANY),
        ],
        out_specs=(pl.BlockSpec(memory_space=pl.ANY), pl.BlockSpec(memory_space=pl.ANY)),
        out_shape=(out, out),
        scratch_shapes=[
            pltpu.VMEM(w_hi.shape, jnp.bfloat16),
            pltpu.VMEM(w_lo.shape, jnp.bfloat16),
            pltpu.VMEM((2, chunks, layers, rows, wide), jnp.float32),
            field,
            field,
            pltpu.VMEM((layers + 2, 2 * rows, wide), jnp.bfloat16),
            halo,
            halo,
            dma((2,)),
            dma((chunks,)),
            dma((chunks, peers)),
            dma((chunks, peers)),
            dma((DEGREE, chunks)),
            dma((DEGREE, chunks)),
            dma((DEGREE, chunks)),
            dma((DEGREE, chunks)),
            dma((2, chunks, peers)),
            dma((2, chunks, peers)),
            dma((2, chunks)),
        ],
        compiler_params=pltpu.CompilerParams(
            collective_id=0, has_side_effects=True, vmem_limit_bytes=VMEM_LIMIT
        ),
    )(src, w_hi, w_lo)

    def back(value):
        value = value.reshape(peers, chunks, layers, lc, face, blk)
        return value.transpose(2, 4, 5, 0, 1, 3).reshape(layers, face, blk, modes_dev)

    return back(x), back(r)


def solution(mesh):
    in_specs = (
        P("space", None, None, "mode"),
        P("space", None, None, None),
        P(None, "space", None, None, None),
        P("space", None, None),
        P(),
    )
    out_specs = (P("space", None, None, "mode"), P("space", None, None, "mode"))
    return jax.shard_map(
        functools.partial(per_device, mesh.shape["mode"], mesh.shape["space"]),
        mesh=mesh, in_specs=in_specs, out_specs=out_specs, check_vma=False,
    )
```

time: 530 us -> 154 us (0.29); the launches traced: 523 us -> 154 us
  waiting for transfers between devices: 217 us -> 0 us
  matrix products: 191 us -> 0 us
  Pallas kernels: 0 us -> 144 us
  local copies, waits for them, and re-layouts: 61.4 us -> 8.52 us
  starting transfers between devices: 35.6 us -> 0 us
  other arithmetic: 16.4 us -> 0 us
    ppermute x20 -> x0, waiting for transfers between devices: 217 us -> none  [the longest x12 181 us: swapped(): return lax.ppermute(value, axis, pairs)]
    dot_general x8 -> x0, matrix products: 191 us -> none  [the longest x4 128 us: operate_on(): jnp.einsum('jlfik,lfkm->jlfim', field_operators, columns, precision=lax.P...]
    pallas_call x0 -> x2, Pallas kernels: none -> 144 us  [the longest x1 129 us: per_device(): pl.pallas_call(functools.partial(solve_kernel, peers, spaces, chunks), in...]
    ppermute x20 -> x0, starting transfers between devices: 35.6 us -> none  [the longest x4 18.1 us: padded_2(): lax.ppermute(head, axis, [((i + 1) % count, i) for i in range(ends)])]
    gather x12 -> x0, local copies, waits for them, and re-layouts: 34.4 us -> none  [gather_columns(): slab_layer[neighbours]]
    unnamed x7 -> x5, local copies, waits for them, and re-layouts: 17.5 us -> 4.18 us
    concatenate x4 -> x0, other arithmetic: 10.2 us -> none  [gather_columns(): jnp.concatenate([centre[:, :, None], lower_layer[:, :, None], upper_layer...]
    broadcast_in_dim x4 -> x0, other arithmetic: 5.51 us -> none  [gather_columns(): lower_layer[:, :, None]]
  transfers between devices with their start and end apart: 20 -> 0, of which waited for: 14 -> 0; matrix products, arithmetic and copies ran while one was open for 7% -> 0% of each run, Pallas kernels for 0% -> 0%
where the time goes in v1:
time: 154 us
  Pallas kernels  144 us (94%)
  local copies, waits for them, and re-layouts  8.52 us (6%)
    pallas_call x1, Pallas kernels, per_device(): pl.pallas_call(functools.partial(solve_kernel, peers, spaces, chunks), in...  129 us
    pallas_call x1, Pallas kernels, prepared(): pl.pallas_call(functools.partial(prep_kernel, face, bits, modes_dev), gri...  15.7 us
    unnamed x5, local copies, waits for them, and re-layouts  4.18 us

profile of v1, /device:TPU:29, one launch (start us, length us, event | category | flops | bytes accessed | tf_op | source)
XLA Modules:
  0.0 153.6 jit_solution(2781595662581724059)
XLA Ops:
  0.6 1.5 %copy.10 = f32[2,4,128,256]{2,3,1,0:T(8,128)S(1)} copy(f32[2,4,128,256]{3,2,1,0:T(8,128)} %param.5) | data formatting | bytes 2097152 | tf_op args[0]
  2.2 0.7 copy.11
  2.9 1.4 reshape.23.src
  4.3 15.7 %shard_map.68 = (bf16[2,4,512,768]{3,2,1,0:T(8,128)(2,1)}, bf16[2,4,512,768]{3,2,1,0:T(8,128)(2,1)}) custom-call(f32[2,4,128,896]{3,2,1,0:T(8,128)} %mean_ref.1, f32[4,2,4,128,896]{4,3,2,1,0:T(8,128)} %field_ref.1, s32[2,4,4]{2,1,0:T(4,128)} %adj_ref.1, s32[4]{0:T(128)} %mask_ref.1), custom_call_target="tpu_custom_call" | custom-call | tf_op jit(solution)/shard_map/pallas_call | solution.py:53
  20.0 128.7 %shard_map.69 = (f32[8,2,2,16,512]{4,3,2,1,0:T(8,128)}, f32[8,2,2,16,512]{4,3,2,1,0:T(8,128)}) custom-call(f32[8,2,2,16,512]{4,3,2,1,0:T(8,128)} %reshape.23.src, bf16[2,4,512,768]{3,2,1,0:T(8,128)(2,1)} %get-tuple-element.6.hi_hbm, bf16[2,4,512,768]{3,2,1,0:T(8,128)(2,1)} %get-tuple-element.7.lo_hbm), custom_call_target="tpu_custom_call" | custom-call | tf_op jit(solution)/shard_map/pallas_call | solution.py:300
  148.6 0.0 copy-start
  148.6 1.7 %reshape.24 = f32[8,2,2,16,4,128]{5,4,3,2,1,0:T(4,128)S(1)} reshape(f32[8,2,2,16,512]{4,3,2,1,0:T(8,128)} %get-tuple-element.8) | data formatting | bytes 2097152 | tf_op jit(solution)/shard_map/reshape | solution.py:336
  150.3 0.1 copy.12
  150.4 1.3 copy.14
  151.7 0.0 copy-done
  151.7 0.4 reshape.26
  152.1 0.1 copy.13
  152.2 1.3 copy.15
Async XLA Ops:
  148.6 3.1 %copy-start = (f32[8,2,2,16,512]{4,3,2,1,0:T(8,128)S(1)}, f32[8,2,2,16,512]{4,3,2,1,0:T(8,128)}, u32[]{:S(2)}) copy-start(f32[8,2,2,16,512]{4,3,2,1,0:T(8,128)} %get-tuple-element.9) | copy-start | bytes 3145732

commit v2 on v1

--- a/solution.py
+++ b/solution.py
@@ -11,63 +11,52 @@
 COUPLING = 0.5773502691896258
 THETA = 1.0
 DELTA = 0.7
-CHUNKS = 2
+CHUNKS = 4
+GROUP = 2
 VMEM_LIMIT = 66_000_000
 MESH = pl.DeviceIdType.MESH
 
 
-def prep_kernel(face, bits, modes_dev, mean_ref, field_ref, adj_ref, mask_ref, hi_ref, lo_ref):
-    layer, f = pl.program_id(0), pl.program_id(1)
-    blk = mean_ref.shape[2]
-    fields = field_ref.shape[0]
-    for op in range(bits + 1):
+def prepare(raw, e, slot, modes_dev, adj_ref, mask_ref, w_hi, w_lo):
+    face, blk = w_hi.shape[1], raw.shape[2]
+    layer, f = e // face, lax.rem(e, face)
+    for op in range(w_hi.shape[2] // blk):
         if op == 0:
-            whole = mean_ref[0, 0]
+            weights = [None]
         else:
-            whole = jnp.zeros(mean_ref.shape[2:], jnp.float32)
-            for j in range(fields):
-                weight = jnp.where(mask_ref[j] == modes_dev * (1 << (op - 1)), COUPLING, 0.0).astype(jnp.float32)
-                whole = whole + weight * field_ref[j, 0, 0]
-        block = lambda s: whole[:, s * blk : (s + 1) * blk]
+            weights = [
+                jnp.where(mask_ref[j] == modes_dev * (1 << (op - 1)), COUPLING, 0.0).astype(jnp.float32)
+                for j in range(raw.shape[1] - 1)
+            ]
+
+        def block(s):
+            lanes = slice(s * blk, (s + 1) * blk)
+            if op == 0:
+                return raw[slot, 0, :, lanes]
+            total = weights[0] * raw[slot, 1, :, lanes]
+            for j in range(1, len(weights)):
+                total = total + weights[j] * raw[slot, 1 + j, :, lanes]
+            return total
+
+        own = block(0)
+        sides = [block(3 + s) for s in range(adj_ref.shape[2])]
         parts = []
         for g in range(face):
-            total = jnp.where(f == g, 1.0, 0.0).astype(jnp.float32) * block(0)
-            for s in range(adj_ref.shape[2]):
-                here = jnp.where(adj_ref[layer, f, s] == g, 1.0, 0.0).astype(jnp.float32)
-                total = total + here * block(3 + s)
+            total = jnp.where(f == g, 1.0, 0.0).astype(jnp.float32) * own
+            for s, side in enumerate(sides):
+                total = total + jnp.where(adj_ref[layer, f, s] == g, 1.0, 0.0).astype(jnp.float32) * side
             parts.append(total)
         parts += [block(1), block(2)]
         for at, part in enumerate(parts):
             high = part.astype(jnp.bfloat16)
             low = (part - high.astype(jnp.float32)).astype(jnp.bfloat16)
-            hi_ref[0, 0, op * blk : (op + 1) * blk, at * blk : (at + 1) * blk] = high
-            lo_ref[0, 0, op * blk : (op + 1) * blk, at * blk : (at + 1) * blk] = low
-
-
-def prepared(mean_operator, field_operators, adjacency, mode_masks, bits, modes_dev):
-    layers, face, blk, wide = mean_operator.shape
-    fields = field_operators.shape[0]
-    shape = (layers, face, (bits + 1) * blk, (face + 2) * blk)
-    out = jax.ShapeDtypeStruct(shape, jnp.bfloat16)
-    spec = pl.BlockSpec((1, 1) + shape[2:], lambda l, f: (l, f, 0, 0))
-    return pl.pallas_call(
-        functools.partial(prep_kernel, face, bits, modes_dev),
-        grid=(layers, face),
-        in_specs=[
-            pl.BlockSpec((1, 1, blk, wide), lambda l, f: (l, f, 0, 0)),
-            pl.BlockSpec((fields, 1, 1, blk, wide), lambda l, f: (0, l, f, 0, 0)),
-            pl.BlockSpec(memory_space=pltpu.SMEM),
-            pl.BlockSpec(memory_space=pltpu.SMEM),
-        ],
-        out_specs=(spec, spec),
-        out_shape=(out, out),
-        compiler_params=pltpu.CompilerParams(vmem_limit_bytes=VMEM_LIMIT),
-    )(mean_operator, field_operators, adjacency, mode_masks)
+            w_hi[layer, f, op * blk : (op + 1) * blk, at * blk : (at + 1) * blk] = high
+            w_lo[layer, f, op * blk : (op + 1) * blk, at * blk : (at + 1) * blk] = low
 
 
 def solve_kernel(
-    peers, spaces, chunks, src, hi_hbm, lo_hbm, x_out, r_out,
-    w_hi, w_lo, direction, res, x, split, halo_low, halo_up,
+    peers, spaces, chunks, modes_dev, src, mean, fields, adj, masks, x_out, r_out,
+    raw, w_hi, w_lo, direction, res, x, split, halo_low, halo_up,
     w_sem, own_sem, in_send, in_recv, low_send, low_recv, up_send, up_recv, out_send, out_recv, own_out,
 ):
     layers, face = w_hi.shape[:2]
@@ -80,10 +69,19 @@
     has_low = s > 0
     has_up = s < spaces - 1
 
-    load_hi = pltpu.make_async_copy(hi_hbm, w_hi, w_sem.at[0])
-    load_lo = pltpu.make_async_copy(lo_hbm, w_lo, w_sem.at[1])
-    load_hi.start()
-    load_lo.start()
+    elements = layers * face
+
+    def loads(e):
+        slot = lax.rem(e, 2)
+        l, f = e // face, lax.rem(e, face)
+        return (
+            pltpu.make_async_copy(mean.at[l, f], raw.at[slot, 0], w_sem.at[slot, 0]),
+            pltpu.make_async_copy(fields.at[:, l, f], raw.at[slot, pl.ds(1, fields.shape[0])], w_sem.at[slot, 1]),
+        )
+
+    for e in range(2):
+        for load in loads(e):
+            load.start()
 
     barrier = pltpu.get_barrier_semaphore()
     for k in range(1, peers):
@@ -201,15 +199,33 @@
     def _():
         halo_up[...] = jnp.zeros_like(halo_up)
 
-    for c in range(chunks):
+    def arrive(c):
         own_copy(c).wait()
         for k in range(1, peers):
             in_wait(c, k)
         halo_start(0, c)
         res[c] = direction[0, c]
         x[c] = direction[0, c]
-    load_hi.wait()
-    load_lo.wait()
+
+    def build(e, carry):
+        for load in loads(e):
+            load.wait()
+        prepare(raw, e, lax.rem(e, 2), modes_dev, adj, masks, w_hi, w_lo)
+
+        @pl.when(e + 2 < elements)
+        def _():
+            for load in loads(e + 2):
+                load.start()
+
+        @pl.when(e == elements // 2)
+        def _():
+            arrive(0)
+
+        return carry
+
+    lax.fori_loop(0, elements, build, 0)
+    for c in range(1, min(GROUP, chunks)):
+        arrive(c)
 
     def keep_split(at, value):
         high = value.astype(jnp.bfloat16)
@@ -221,11 +237,21 @@
 
     sigma = THETA / DELTA
 
-    def step(i, ratio):
-        t, c = i // chunks, lax.rem(i, chunks)
+    ratios = [1.0 / sigma]
+    for _ in range(DEGREE):
+        ratios.append(1.0 / (2.0 * sigma - ratios[-1]))
+    group = min(GROUP, chunks)
+    per_group = DEGREE * group
+
+    def step(i, carry):
+        within = lax.rem(i, per_group)
+        t = within // group
+        c = (i // per_group) * group + lax.rem(within, group)
         now = lax.rem(t, 2)
-        ratio_new = 1.0 / (2.0 * sigma - ratio)
-        keep, add = ratio_new * ratio, 2.0 * ratio_new / DELTA
+        keep, add = jnp.float32(0.0), jnp.float32(0.0)
+        for at in range(DEGREE):
+            keep = jnp.where(t == at, jnp.float32(ratios[at + 1] * ratios[at]), keep)
+            add = jnp.where(t == at, jnp.float32(2.0 * ratios[at + 1] / DELTA), add)
         for l in range(layers):
             keep_split(l + 1, direction[now, c, l])
         halo_arrived(t, c)
@@ -270,9 +296,13 @@
         def _():
             out_start(1, res, r_out, c)
 
-        return jnp.where(c == chunks - 1, ratio_new, ratio)
-
-    lax.fori_loop(0, DEGREE * chunks, step, jnp.float32(1.0 / sigma))
+        @pl.when(jnp.logical_and(t == DEGREE - 2, c + group < chunks))
+        def _():
+            arrive(c + group)
+
+        return carry
+
+    lax.fori_loop(0, DEGREE * chunks, step, 0)
 
     for c in range(chunks):
         halo_sent(DEGREE - 1, c)
@@ -287,10 +317,12 @@
     layers, face, blk, modes_dev = source_field.shape
     bits = peers.bit_length() - 1
     chunks = CHUNKS
+    while modes_dev % (peers * chunks * 8):
+        chunks //= 2
     lc = modes_dev // (peers * chunks)
     rows = peers * lc
     wide = face * blk
-    w_hi, w_lo = prepared(mean_operator, field_operators, adjacency, mode_masks, bits, modes_dev)
+    weights = pltpu.VMEM((layers, face, (bits + 1) * blk, (face + 2) * blk), jnp.bfloat16)
     src = source_field.reshape(layers, face, blk, peers, chunks, lc)
     src = src.transpose(3, 4, 0, 5, 1, 2).reshape(peers, chunks, layers, lc, wide) / THETA
     out = jax.ShapeDtypeStruct(src.shape, jnp.float32)
@@ -298,24 +330,27 @@
     halo = pltpu.VMEM((DEGREE, chunks, rows, wide), jnp.float32)
     dma = pltpu.SemaphoreType.DMA
     x, r = pl.pallas_call(
-        functools.partial(solve_kernel, peers, spaces, chunks),
+        functools.partial(solve_kernel, peers, spaces, chunks, modes_dev),
         in_specs=[
             pl.BlockSpec(memory_space=pltpu.VMEM),
             pl.BlockSpec(memory_space=pl.ANY),
             pl.BlockSpec(memory_space=pl.ANY),
+            pl.BlockSpec(memory_space=pltpu.SMEM),
+            pl.BlockSpec(memory_space=pltpu.SMEM),
         ],
         out_specs=(pl.BlockSpec(memory_space=pl.ANY), pl.BlockSpec(memory_space=pl.ANY)),
         out_shape=(out, out),
         scratch_shapes=[
-            pltpu.VMEM(w_hi.shape, jnp.bfloat16),
-            pltpu.VMEM(w_lo.shape, jnp.bfloat16),
+            pltpu.VMEM((2, 1 + field_operators.shape[0]) + mean_operator.shape[2:], jnp.float32),
+            weights,
+            weights,
             pltpu.VMEM((2, chunks, layers, rows, wide), jnp.float32),
             field,
             field,
             pltpu.VMEM((layers + 2, 2 * rows, wide), jnp.bfloat16),
             halo,
             halo,
-            dma((2,)),
+            dma((2, 2)),
             dma((chunks,)),
             dma((chunks, peers)),
             dma((chunks, peers)),
@@ -330,7 +365,7 @@
         compiler_params=pltpu.CompilerParams(
             collective_id=0, has_side_effects=True, vmem_limit_bytes=VMEM_LIMIT
         ),
-    )(src, w_hi, w_lo)
+    )(src, mean_operator, field_operators, adjacency, mode_masks)
 
     def back(value):
         value = value.reshape(peers, chunks, layers, lc, face, blk)

time: 154 us -> 139 us (0.903)
  Pallas kernels: 144 us -> 128 us
    pallas_call x2 -> x1, Pallas kernels: 144 us -> 128 us  [per_device(): pl.pallas_call(functools.partial(solve_kernel, peers, spaces, chunks, mod...]
    unnamed x5 -> x3, local copies, waits for them, and re-layouts: 4.18 us -> 4.18 us
where the time goes in v2:
time: 139 us; the launch traced here: 137 us
  Pallas kernels  128 us (92%)
  local copies, waits for them, and re-layouts  7.99 us (6%)
    pallas_call x1, Pallas kernels, per_device(): pl.pallas_call(functools.partial(solve_kernel, peers, spaces, chunks, mod...  128 us
    unnamed x3, local copies, waits for them, and re-layouts  4.18 us

profile of v2, /device:TPU:29, one launch (start us, length us, event | category | flops | bytes accessed | tf_op | source)
XLA Modules:
  0.0 137.0 jit_solution(11544317467879528971)
XLA Ops:
  0.6 1.5 %copy.10 = f32[2,4,128,256]{2,3,1,0:T(8,128)S(1)} copy(f32[2,4,128,256]{3,2,1,0:T(8,128)} %param.5) | data formatting | bytes 2097152 | tf_op args[0]
  2.2 1.1 copy.17
  3.3 128.4 %shard_map.68 = (f32[8,4,2,8,512]{4,3,2,1,0:T(8,128)}, f32[8,4,2,8,512]{4,3,2,1,0:T(8,128)}) custom-call(f32[8,4,2,8,512]{4,3,2,1,0:T(8,128)} %bitcast.14, f32[2,4,128,896]{3,2,1,0:T(8,128)} %mean.1, f32[4,2,4,128,896]{4,3,2,1,0:T(8,128)} %fields.1, s32[2,4,4]{2,1,0:T(4,128)} %adj.1, s32[4]{0:T(128)} %masks.1), custom_call_target="tpu_custom_call" | custom-call | tf_op jit(solution)/shard_map/pallas_call | solution.py:332
  131.7 1.4 copy.12
  133.1 1.3 copy.14
  134.4 1.4 copy.13
  135.7 1.3 copy.15

commit v3 on v2

--- a/solution.py
+++ b/solution.py
@@ -13,6 +13,9 @@
 DELTA = 0.7
 CHUNKS = 4
 GROUP = 2
+LAG = 2
+SLOTS = 4
+Y_FIRST = True
 VMEM_LIMIT = 66_000_000
 MESH = pl.DeviceIdType.MESH
 
@@ -20,7 +23,7 @@
 def prepare(raw, e, slot, modes_dev, adj_ref, mask_ref, w_hi, w_lo):
     face, blk = w_hi.shape[1], raw.shape[2]
     layer, f = e // face, lax.rem(e, face)
-    for op in range(w_hi.shape[2] // blk):
+    for op in range(w_hi.shape[3] // blk):
         if op == 0:
             weights = [None]
         else:
@@ -48,19 +51,21 @@
             parts.append(total)
         parts += [block(1), block(2)]
         for at, part in enumerate(parts):
+            part = part.T
             high = part.astype(jnp.bfloat16)
             low = (part - high.astype(jnp.float32)).astype(jnp.bfloat16)
-            w_hi[layer, f, op * blk : (op + 1) * blk, at * blk : (at + 1) * blk] = high
-            w_lo[layer, f, op * blk : (op + 1) * blk, at * blk : (at + 1) * blk] = low
+            w_hi[layer, f, at * blk : (at + 1) * blk, op * blk : (op + 1) * blk] = high
+            w_lo[layer, f, at * blk : (at + 1) * blk, op * blk : (op + 1) * blk] = low
 
 
 def solve_kernel(
     peers, spaces, chunks, modes_dev, src, mean, fields, adj, masks, x_out, r_out,
-    raw, w_hi, w_lo, direction, res, x, split, halo_low, halo_up,
-    w_sem, own_sem, in_send, in_recv, low_send, low_recv, up_send, up_recv, out_send, out_recv, own_out,
+    raw, w_hi, w_lo, direction, res, x, split, halo_low, halo_up, relay,
+    w_sem, own_sem, in_send, in_recv, low_send, low_recv, up_send, up_recv,
+    relay_send, relay_recv, forward_send, forward_recv, out_send, out_recv, own_out,
 ):
     layers, face = w_hi.shape[:2]
-    blk = w_hi.shape[2] // (peers.bit_length())
+    blk = w_hi.shape[3] // (peers.bit_length())
     bits = peers.bit_length() - 1
     lc = src.shape[3]
     rows = peers * lc
@@ -68,18 +73,22 @@
     s = lax.axis_index("space")
     has_low = s > 0
     has_up = s < spaces - 1
+    relayed = spaces >= 4 and spaces % 2 == 0
+    odd = lax.rem(s, 2) == 1
+    even = jnp.logical_not(odd)
+    half = rows // 2 if relayed else rows
 
     elements = layers * face
 
     def loads(e):
-        slot = lax.rem(e, 2)
+        slot = lax.rem(e, SLOTS)
         l, f = e // face, lax.rem(e, face)
         return (
             pltpu.make_async_copy(mean.at[l, f], raw.at[slot, 0], w_sem.at[slot, 0]),
             pltpu.make_async_copy(fields.at[:, l, f], raw.at[slot, pl.ds(1, fields.shape[0])], w_sem.at[slot, 1]),
         )
 
-    for e in range(2):
+    for e in range(min(SLOTS, elements)):
         for load in loads(e):
             load.start()
 
@@ -95,7 +104,20 @@
     def _():
         pl.semaphore_signal(barrier, inc=1, device_id={"space": s + 1}, device_id_type=MESH)
 
-    pl.semaphore_wait(barrier, peers - 1 + has_low.astype(jnp.int32) + has_up.astype(jnp.int32))
+    expected = peers - 1 + has_low.astype(jnp.int32) + has_up.astype(jnp.int32)
+    if relayed:
+        far_low, far_up = s >= 2, s < spaces - 2
+        expected = expected + far_low.astype(jnp.int32) + far_up.astype(jnp.int32)
+
+        @pl.when(far_low)
+        def _():
+            pl.semaphore_signal(barrier, inc=1, device_id={"space": s - 2}, device_id_type=MESH)
+
+        @pl.when(far_up)
+        def _():
+            pl.semaphore_signal(barrier, inc=1, device_id={"space": s + 2}, device_id_type=MESH)
+
+    pl.semaphore_wait(barrier, expected)
 
     def slab(ref, c, h):
         return ref.at[c, :, pl.ds(pl.multiple_of(h * lc, lc), lc), :]
@@ -118,46 +140,120 @@
     def own_copy(c):
         return pltpu.make_async_copy(src.at[me, c], slab(direction.at[0], c, me), own_sem.at[c])
 
-    def to_low(t, c):
+    def to_low(t, c, count):
         return pltpu.make_async_remote_copy(
-            src_ref=direction.at[lax.rem(t, 2), c, 0], dst_ref=halo_up.at[t, c],
+            src_ref=direction.at[lax.rem(t, 2), c, 0, pl.ds(0, count)], dst_ref=halo_up.at[t, c, pl.ds(0, count)],
             send_sem=low_send.at[t, c], recv_sem=up_recv.at[t, c],
             device_id={"space": s - 1}, device_id_type=MESH,
         )
 
-    def to_up(t, c):
+    def to_up(t, c, count):
         return pltpu.make_async_remote_copy(
-            src_ref=direction.at[lax.rem(t, 2), c, layers - 1], dst_ref=halo_low.at[t, c],
+            src_ref=direction.at[lax.rem(t, 2), c, layers - 1, pl.ds(0, count)],
+            dst_ref=halo_low.at[t, c, pl.ds(0, count)],
             send_sem=up_send.at[t, c], recv_sem=low_recv.at[t, c],
             device_id={"space": s + 1}, device_id_type=MESH,
         )
 
+    def to_relay(t, c, layer, offset):
+        return pltpu.make_async_remote_copy(
+            src_ref=direction.at[lax.rem(t, 2), c, layer, pl.ds(half, rows - half)], dst_ref=relay.at[t, c],
+            send_sem=relay_send.at[t, c], recv_sem=relay_recv.at[t, c],
+            device_id={"space": s + offset}, device_id_type=MESH,
+        )
+
+    def forward(t, c, halo, offset):
+        return pltpu.make_async_remote_copy(
+            src_ref=relay.at[t, c], dst_ref=halo.at[t, c, pl.ds(half, rows - half)],
+            send_sem=forward_send.at[t, c], recv_sem=forward_recv.at[t, c],
+            device_id={"space": s + offset}, device_id_type=MESH,
+        )
+
+    both = jnp.logical_and
+    up_offset, low_offset = (2, -2) if Y_FIRST else (-1, 1)
+    if relayed:
+        whole_low, whole_up = both(odd, has_low), both(even, has_up)
+        part_low, part_up = both(even, has_low), both(odd, has_up)
+    else:
+        whole_low, whole_up = has_low, has_up
+
+    def halo_each(t, c, act):
+        @pl.when(whole_low)
+        def _():
+            act(to_low(t, c, rows))
+
+        @pl.when(whole_up)
+        def _():
+            act(to_up(t, c, rows))
+
+        if relayed:
+
+            @pl.when(part_low)
+            def _():
+                act(to_relay(t, c, 0, low_offset))
+                act(to_low(t, c, half))
+
+            @pl.when(part_up)
+            def _():
+                act(to_relay(t, c, layers - 1, up_offset))
+                act(to_up(t, c, half))
+
     def halo_start(t, c):
-        @pl.when(has_low)
-        def _():
-            to_low(t, c).start()
-
-        @pl.when(has_up)
-        def _():
-            to_up(t, c).start()
+        halo_each(t, c, lambda copy: copy.start())
 
     def halo_sent(t, c):
-        @pl.when(has_low)
-        def _():
-            to_low(t, c).wait_send()
-
-        @pl.when(has_up)
-        def _():
-            to_up(t, c).wait_send()
+        halo_each(t, c, lambda copy: copy.wait_send())
+
+    def forward_each(t, c, act):
+        if relayed:
+
+            @pl.when(both(odd, s >= 3))
+            def _():
+                act(forward(t, c, *((halo_low, -1) if Y_FIRST else (halo_up, -2))))
+
+            @pl.when(both(even, s < spaces - 3))
+            def _():
+                act(forward(t, c, *((halo_up, 1) if Y_FIRST else (halo_low, 2))))
+
+    def halo_forward(t, c):
+        if relayed:
+
+            @pl.when(jnp.logical_or(both(odd, s >= 3), both(even, s < spaces - 3)))
+            def _():
+                to_relay(t, c, 0, jnp.where(odd, -1, 1)).wait_recv()
+
+            forward_each(t, c, lambda copy: copy.start())
 
     def halo_arrived(t, c):
-        @pl.when(has_low)
-        def _():
-            to_up(t, c).wait_recv()
-
-        @pl.when(has_up)
-        def _():
-            to_low(t, c).wait_recv()
+        if not relayed:
+
+            @pl.when(has_low)
+            def _():
+                to_up(t, c, rows).wait_recv()
+
+            @pl.when(has_up)
+            def _():
+                to_low(t, c, rows).wait_recv()
+
+            return
+
+        @pl.when(both(odd, has_low))
+        def _():
+            to_up(t, c, rows).wait_recv()
+
+        @pl.when(both(even, has_up))
+        def _():
+            to_low(t, c, rows).wait_recv()
+
+        @pl.when(both(even, has_low))
+        def _():
+            to_up(t, c, half).wait_recv()
+            forward(t, c, halo_low, -1).wait_recv()
+
+        @pl.when(both(odd, has_up))
+        def _():
+            to_low(t, c, half).wait_recv()
+            forward(t, c, halo_up, 1).wait_recv()
 
     def out_copy(which, ref, out, c, k):
         to = lax.rem(me + k, peers)
@@ -210,11 +306,11 @@
     def build(e, carry):
         for load in loads(e):
             load.wait()
-        prepare(raw, e, lax.rem(e, 2), modes_dev, adj, masks, w_hi, w_lo)
-
-        @pl.when(e + 2 < elements)
-        def _():
-            for load in loads(e + 2):
+        prepare(raw, e, lax.rem(e, SLOTS), modes_dev, adj, masks, w_hi, w_lo)
+
+        @pl.when(e + SLOTS < elements)
+        def _():
+            for load in loads(e + SLOTS):
                 load.start()
 
         @pl.when(e == elements // 2)
@@ -224,7 +320,8 @@
         return carry
 
     lax.fori_loop(0, elements, build, 0)
-    for c in range(1, min(GROUP, chunks)):
+    group = min(GROUP, chunks)
+    for c in range(1, group):
         arrive(c)
 
     def keep_split(at, value):
@@ -233,20 +330,31 @@
         split[at, rows:, :] = (value - high.astype(jnp.float32)).astype(jnp.bfloat16)
 
     def product(a, b):
-        return lax.dot_general(a, b, (((1,), (1,)), ((), ())), preferred_element_type=jnp.float32)
+        return lax.dot_general(a, b, (((1,), (0,)), ((), ())), preferred_element_type=jnp.float32)
 
     sigma = THETA / DELTA
 
     ratios = [1.0 / sigma]
     for _ in range(DEGREE):
         ratios.append(1.0 / (2.0 * sigma - ratios[-1]))
-    group = min(GROUP, chunks)
-    per_group = DEGREE * group
+    order = []
+    arrivals = {}
+    for turn in range(DEGREE + LAG * (chunks // group - 1)):
+        for place in range(group):
+            for c in range(place, chunks, group):
+                t = turn - LAG * (c // group)
+                if 0 <= t < DEGREE:
+                    order.append((t, c))
+        for c in range(group, chunks):
+            if turn == max(LAG * (c // group) - 1, 0):
+                arrivals[c] = len(order) - 1
+
 
     def step(i, carry):
-        within = lax.rem(i, per_group)
-        t = within // group
-        c = (i // per_group) * group + lax.rem(within, group)
+        t, c = jnp.int32(0), jnp.int32(0)
+        for at, (t_at, c_at) in enumerate(order):
+            t = jnp.where(i == at, t_at, t)
+            c = jnp.where(i == at, c_at, c)
         now = lax.rem(t, 2)
         keep, add = jnp.float32(0.0), jnp.float32(0.0)
         for at in range(DEGREE):
@@ -254,6 +362,7 @@
             add = jnp.where(t == at, jnp.float32(2.0 * ratios[at + 1] / DELTA), add)
         for l in range(layers):
             keep_split(l + 1, direction[now, c, l])
+        halo_forward(t, c)
         halo_arrived(t, c)
         keep_split(0, halo_low[t, c])
         keep_split(layers + 1, halo_up[t, c])
@@ -296,9 +405,11 @@
         def _():
             out_start(1, res, r_out, c)
 
-        @pl.when(jnp.logical_and(t == DEGREE - 2, c + group < chunks))
-        def _():
-            arrive(c + group)
+        for late, at in arrivals.items():
+
+            @pl.when(i == at)
+            def _():
+                arrive(late)
 
         return carry
 
@@ -306,6 +417,8 @@
 
     for c in range(chunks):
         halo_sent(DEGREE - 1, c)
+        for t in range(DEGREE):
+            forward_each(t, c, lambda copy: copy.wait_send())
         for k in range(1, peers):
             in_copy(c, k).wait_send()
     for c in range(chunks):
@@ -322,7 +435,7 @@
     lc = modes_dev // (peers * chunks)
     rows = peers * lc
     wide = face * blk
-    weights = pltpu.VMEM((layers, face, (bits + 1) * blk, (face + 2) * blk), jnp.bfloat16)
+    weights = pltpu.VMEM((layers, face, (face + 2) * blk, (bits + 1) * blk), jnp.bfloat16)
     src = source_field.reshape(layers, face, blk, peers, chunks, lc)
     src = src.transpose(3, 4, 0, 5, 1, 2).reshape(peers, chunks, layers, lc, wide) / THETA
     out = jax.ShapeDtypeStruct(src.shape, jnp.float32)
@@ -341,7 +454,7 @@
         out_specs=(pl.BlockSpec(memory_space=pl.ANY), pl.BlockSpec(memory_space=pl.ANY)),
         out_shape=(out, out),
         scratch_shapes=[
-            pltpu.VMEM((2, 1 + field_operators.shape[0]) + mean_operator.shape[2:], jnp.float32),
+            pltpu.VMEM((SLOTS, 1 + field_operators.shape[0]) + mean_operator.shape[2:], jnp.float32),
             weights,
             weights,
             pltpu.VMEM((2, chunks, layers, rows, wide), jnp.float32),
@@ -350,10 +463,15 @@
             pltpu.VMEM((layers + 2, 2 * rows, wide), jnp.bfloat16),
             halo,
             halo,
-            dma((2, 2)),
+            pltpu.VMEM((DEGREE, chunks, rows // 2, wide), jnp.float32),
+            dma((SLOTS, 2)),
             dma((chunks,)),
             dma((chunks, peers)),
             dma((chunks, peers)),
+            dma((DEGREE, chunks)),
+            dma((DEGREE, chunks)),
+            dma((DEGREE, chunks)),
+            dma((DEGREE, chunks)),
             dma((DEGREE, chunks)),
             dma((DEGREE, chunks)),
             dma((DEGREE, chunks)),

time: 139 us -> 125 us (0.90)
  Pallas kernels: 128 us -> 115 us
    pallas_call x1, Pallas kernels: 128 us -> 115 us  [per_device(): pl.pallas_call(functools.partial(solve_kernel, peers, spaces, chunks, mod...]
where the time goes in v3:
time: 125 us; the launch traced here: 123 us
  Pallas kernels  115 us (92%)
  local copies, waits for them, and re-layouts  7.99 us (6%)
    pallas_call x1, Pallas kernels, per_device(): pl.pallas_call(functools.partial(solve_kernel, peers, spaces, chunks, mod...  115 us
    unnamed x3, local copies, waits for them, and re-layouts  4.18 us
    reshape x2, local copies, waits for them, and re-layouts, back(): value = value.reshape(peers, chunks, layers, lc, face, blk)  2.7 us

profile of v3, /device:TPU:29, one launch (start us, length us, event | category | flops | bytes accessed | tf_op | source)
XLA Modules:
  0.0 123.5 jit_solution(5050326728101110632)
XLA Ops:
  0.6 1.5 %copy.10 = f32[2,4,128,256]{2,3,1,0:T(8,128)S(1)} copy(f32[2,4,128,256]{3,2,1,0:T(8,128)} %param.5) | data formatting | bytes 2097152 | tf_op args[0]
  2.2 1.1 copy.17
  3.3 114.8 %shard_map.68 = (f32[8,4,2,8,512]{4,3,2,1,0:T(8,128)}, f32[8,4,2,8,512]{4,3,2,1,0:T(8,128)}) custom-call(f32[8,4,2,8,512]{4,3,2,1,0:T(8,128)} %bitcast.14, f32[2,4,128,896]{3,2,1,0:T(8,128)} %mean.1, f32[4,2,4,128,896]{4,3,2,1,0:T(8,128)} %fields.1, s32[2,4,4]{2,1,0:T(4,128)} %adj.1, s32[4]{0:T(128)} %masks.1), custom_call_target="tpu_custom_call" | custom-call | tf_op jit(solution)/shard_map/pallas_call | solution.py:445
  118.1 1.4 %copy.12 = f32[8,4,2,8,4,128]{5,3,1,0,4,2:T(8,128)S(1)} copy(f32[8,4,2,8,4,128]{5,3,4,2,1,0:T(8,128)} %bitcast.19) | data formatting | bytes 2097152 | tf_op jit(solution)/shard_map/reshape | solution.py:489
  119.5 1.3 %copy.14 = f32[2,4,128,256]{3,2,1,0:T(8,128)} copy(f32[2,4,128,256]{2,3,1,0:T(8,128)S(1)} %bitcast.15) | data formatting | bytes 2097152
  120.8 1.4 %copy.13 = f32[8,4,2,8,4,128]{5,3,1,0,4,2:T(8,128)S(1)} copy(f32[8,4,2,8,4,128]{5,3,4,2,1,0:T(8,128)} %bitcast.18) | data formatting | bytes 2097152 | tf_op jit(solution)/shard_map/reshape | solution.py:489
  122.2 1.3 %copy.15 = f32[2,4,128,256]{3,2,1,0:T(8,128)} copy(f32[2,4,128,256]{2,3,1,0:T(8,128)S(1)} %bitcast.16) | data formatting | bytes 2097152
